TPU v7x, 512 devices: a whole 4x4x16 slice. The times are simulated.
512 devices in a mesh: row: 32 (over z_hi, x, core), col: 16 (over y, z_lo).
Axes of the slice: x: 4, y: 4, z: 16 (z_hi: 4, z_lo: 4; z = z_hi * 4 + z_lo), core: 2. Of those that a mesh axis runs over, the one named last changes fastest.
Arguments:
- right_sides: float32 [8, 131072], P(None, ('row', 'col')), may hold values from -11 to 11
- noise_var: float32 [131072], P(('row', 'col')), may hold values from 1.2 to 3
- observed: int32 [131072], P(('row', 'col')), may hold values 0 or 1
- tile_data: bfloat16 [32, 16, 32, 128, 128], P('row', 'col'), may hold values from -1 to 1
- diag_tiles: bfloat16 [1024, 128, 128], P(('row', 'col')), may hold values from -1 to 1
- tile_rows: int32 [32, 16, 32], P('row', 'col'), may hold values from 0 to 63
- tile_cols: int32 [32, 16, 32], P('row', 'col'), may hold values from 0 to 31
- tile_count: int32 [32, 16], P('row', 'col'), may hold values from 16 to 32, as said below
Outputs:
- solution: float32 [8, 131072], P(None, ('row', 'col'))
- residual: float32 [8, 131072], P(None, ('row', 'col'))
Inputs may be any that keep to these rules, and one draw needn't show every extreme that they name: A device's slots t < tile_count name distinct pairs (i, j) whose blocks satisfy I != J, with I < J exactly when I + J is even, so that each pair of blocks is stored at most once; slots beyond the count hold arbitrary indices in range. Every device of the last row has exactly 32 live slots.
All inputs are finite; a program needn't handle non-finite values. No bound on the sum of `observed` on one device may be relied on, other than what follows from the above.
Results may differ from a plain program's by a relative error of at most 0.0003.
Values sent between devices are 32-bit elements; how exact they have to be, the bound alone decides.
A program may use at most 64 MiB of HBM per device.

v0:
```python
import math
import jax
import jax.numpy as jnp
from jax import lax
from jax.sharding import PartitionSpec as P

TILE = 128
COUPLED = 32
ITERS = 2


def residual_norms(residual):
    return lax.psum(jnp.sum(residual * residual, axis=1), ("row", "col"))


def local(
    right_sides, noise_var, observed, tile_data, diag_tiles, tile_rows, tile_cols, tile_count
):
    rhs_count = right_sides.shape[0]
    block_here = diag_tiles.shape[0]
    tile_size = diag_tiles.shape[1]
    piece_len = block_here * tile_size
    row_devices = lax.axis_size("row")
    col_devices = lax.axis_size("col")
    coupling = 1.0 / (2.0 * math.sqrt(TILE * (2 * COUPLED + 1)))
    highest = lax.Precision.HIGHEST
    observed_float = observed.astype(jnp.float32)[None, :]
    noise_row = noise_var[None, :]
    local_tiles = tile_data[0, 0].astype(jnp.float32)
    picks_row = tile_rows[0, 0]
    picks_col = tile_cols[0, 0]
    live_slots = jnp.arange(local_tiles.shape[0]) < tile_count[0, 0]
    row_hot = (
        (picks_row[:, None] == jnp.arange(row_devices * block_here)[None, :]) & live_slots[:, None]
    ).astype(jnp.float32)
    col_hot = (
        (picks_col[:, None] == jnp.arange(col_devices * block_here)[None, :]) & live_slots[:, None]
    ).astype(jnp.float32)
    row_index = jnp.arange(tile_size)[:, None]
    col_index = jnp.arange(tile_size)[None, :]
    diag_float = diag_tiles.astype(jnp.float32)
    zero_tiles = jnp.zeros_like(diag_float)
    diag_upper = jnp.where((col_index >= row_index)[None, :, :], diag_float, zero_tiles)
    diag_strict = jnp.where((col_index > row_index)[None, :, :], diag_float, zero_tiles)
    solution = jnp.zeros_like(right_sides)
    residual = right_sides
    direction = right_sides
    norm_now = residual_norms(residual)
    for iteration in range(ITERS):
        masked = observed_float * direction
        by_col = lax.all_gather(masked, "col", axis=1, tiled=True)
        by_row = lax.all_gather(masked, "row", axis=1, tiled=True)
        by_col = by_col.reshape(rhs_count, col_devices * block_here, tile_size)
        by_row = by_row.reshape(rhs_count, row_devices * block_here, tile_size)
        upper_terms = jnp.einsum(
            "tab,stb->sta", local_tiles, jnp.take(by_col, picks_col, axis=1), precision=highest
        )
        row_terms = jnp.einsum("sta,ti->sia", upper_terms, row_hot, precision=highest)
        own_rows = lax.psum_scatter(
            row_terms.reshape(rhs_count, row_devices * piece_len),
            "row",
            scatter_dimension=1,
            tiled=True,
        )
        lower_terms = jnp.einsum(
            "tab,sta->stb", local_tiles, jnp.take(by_row, picks_row, axis=1), precision=highest
        )
        col_terms = jnp.einsum("stb,tj->sjb", lower_terms, col_hot, precision=highest)
        mirrored = lax.psum_scatter(
            col_terms.reshape(rhs_count, col_devices * piece_len),
            "col",
            scatter_dimension=1,
            tiled=True,
        )
        local_blocks = masked.reshape(rhs_count, block_here, tile_size)
        diag_terms = jnp.einsum("kab,skb->ska", diag_upper, local_blocks, precision=highest)
        diag_terms = diag_terms + jnp.einsum(
            "kab,ska->skb", diag_strict, local_blocks, precision=highest
        )
        total = own_rows + mirrored + diag_terms.reshape(rhs_count, piece_len)
        image_field = noise_row * direction + observed_float * (coupling * total)
        step_alpha = norm_now / lax.psum(jnp.sum(direction * image_field, axis=1), ("row", "col"))
        solution = solution + step_alpha[:, None] * direction
        residual = residual - step_alpha[:, None] * image_field
        norm_next = residual_norms(residual)
        direction = residual + (norm_next / norm_now)[:, None] * direction
        norm_now = norm_next
    return (solution, residual)


def solution(mesh):
    return jax.shard_map(
        local,
        mesh=mesh,
        in_specs=(
            P(None, ("row", "col")),
            P(("row", "col")),
            P(("row", "col")),
            P("row", "col", None, None, None),
            P(("row", "col"), None, None),
            P("row", "col", None),
            P("row", "col", None),
            P("row", "col"),
        ),
        out_specs=(P(None, ("row", "col")), P(None, ("row", "col"))),
        check_vma=False,
    )
```

profile of v0, /device:TPU:1, one launch (start us, length us, event | category | flops | bytes accessed | tf_op | source)
XLA Modules:
  0.0 862.3 jit_solution(10460393890309216565)
XLA Ops:
  7.2 0.0 copy-start
  7.2 0.0 reduce-scatter.7.cloned.1.call-start
  7.2 0.7 compare_select_fusion
  8.0 0.7 convert_element_type.4
  9.4 61.0 %all_gather.13 = f32[8,8192]{1,0:T(8,128)S(1)} all-gather(f32[8,256]{1,0:T(8,128)S(1)} %broadcast_multiply_fusion.1), channel_id=1, replica_groups=mesh['row'=32,'col'=16] {'row'}, dimensions={1}, use_global_device_ids=true | all-gather | bytes 270336 | tf_op jit(solution)/shard_map/all_gather | solution.py:52
  70.4 0.6 gather_fusion.1
  71.0 1.0 fusion.12
  72.0 0.7 copy-done.3
  72.7 0.2 convolution_bitcast_fusion.3
  72.9 0.7 copy.41
  73.6 0.0 reduce-scatter.7.cloned.1.call-update
  73.6 0.0 reduce-scatter.5.cloned.1.call-start
  73.7 35.8 %all_gather.12 = f32[8,4096]{1,0:T(8,128)S(1)} all-gather(f32[8,256]{1,0:T(8,128)S(1)} %broadcast_multiply_fusion.1), channel_id=1, replica_groups=mesh['row'=32,'col'=16] {'col'}, dimensions={1}, use_global_device_ids=true | all-gather | bytes 139264 | tf_op jit(solution)/shard_map/all_gather | solution.py:51
  109.5 0.6 gather_fusion
  110.1 1.8 fusion.14
  111.8 0.4 convolution_bitcast_fusion.1
  112.2 0.8 copy.39
  113.1 0.0 reduce-scatter.5.cloned.1.call-update
  113.1 0.0 reduce-scatter.11.cloned.1.call-start
  113.2 0.6 copy-done.2
  113.8 0.1 copy-done.5
  114.0 0.3 fusion.17
  114.2 28.7 %reduce-scatter.7.cloned.1.call-done = f32[8,256]{1,0:T(8,128)} async-done(((f32[8,4096]{1,0:T(8,128)}), f32[8,256]{1,0:T(8,128)}) %reduce-scatter.7.cloned.1.call-update) | async-done | bytes 8208 | tf_op jit(solution)/shard_map/reduce_scatter | solution.py:69
  143.0 121.6 %reduce-scatter.5.cloned.1.call-done = f32[8,256]{1,0:T(8,128)} async-done(((f32[8,8192]{1,0:T(8,128)}), f32[8,256]{1,0:T(8,128)}) %reduce-scatter.5.cloned.1.call-update) | async-done | bytes 8208 | tf_op jit(solution)/shard_map/reduce_scatter | solution.py:59
  264.6 1.1 multiply_reduce_fusion.2
  265.7 101.8 %all-reduce = (f32[8]{0:T(128)S(1)}, f32[8]{0:T(128)S(1)}) all-reduce(f32[8]{0:T(128)S(1)} %get-tuple-element.5, f32[8]{0:T(128)S(1)} %get-tuple-element.4), channel_id=1, replica_groups=mesh['row'=32,'col'=16] {'row','col'}, use_global_device_ids=true, to_apply=%region_1.2 | all-reduce | flops 16 | bytes 128 | tf_op jit(solution)/shard_map/psum | solution.py:13
  367.4 0.2 multiply_reduce_fusion.1
  367.6 100.1 %psum.30 = f32[8]{0:T(128)S(1)} all-reduce(f32[8]{0:T(128)S(1)} %multiply_reduce_fusion.1), channel_id=1, replica_groups=mesh['row'=32,'col'=16] {'row','col'}, use_global_device_ids=true, to_apply=%region_7.10 | all-reduce | flops 8 | bytes 64 | tf_op jit(solution)/shard_map/psum | solution.py:13
  467.8 0.1 broadcast_multiply_fusion
  467.9 34.1 %all_gather.14 = f32[8,4096]{1,0:T(8,128)S(1)} all-gather(f32[8,256]{1,0:T(8,128)S(1)} %get-tuple-element.8), channel_id=1, replica_groups=mesh['row'=32,'col'=16] {'col'}, dimensions={1}, use_global_device_ids=true | all-gather | bytes 139264 | tf_op jit(solution)/shard_map/all_gather | solution.py:51
  502.0 57.3 %all_gather.15 = f32[8,8192]{1,0:T(8,128)S(1)} all-gather(f32[8,256]{1,0:T(8,128)S(1)} %get-tuple-element.8), channel_id=1, replica_groups=mesh['row'=32,'col'=16] {'row'}, dimensions={1}, use_global_device_ids=true | all-gather | bytes 270336 | tf_op jit(solution)/shard_map/all_gather | solution.py:52
  559.3 0.6 gather_fusion.2
  559.9 0.6 gather_fusion.3
  560.5 1.0 fusion.8
  561.4 0.2 convolution_bitcast_fusion.2
  561.7 0.7 copy.40
  562.4 0.0 reduce-scatter.11.cloned.1.call-update
  562.4 0.0 reduce-scatter.9.cloned.1.call-start
  562.5 1.8 fusion.10
  564.2 0.4 convolution_bitcast_fusion
  564.6 0.8 copy.38
  565.5 0.0 reduce-scatter.9.cloned.1.call-update
  565.5 0.3 fusion.16
  565.8 64.8 %reduce-scatter.11.cloned.1.call-done = f32[8,256]{1,0:T(8,128)} async-done(((f32[8,4096]{1,0:T(8,128)}), f32[8,256]{1,0:T(8,128)}) %reduce-scatter.11.cloned.1.call-update) | async-done | bytes 8208 | tf_op jit(solution)/shard_map/reduce_scatter | solution.py:69
  630.7 121.7 %reduce-scatter.9.cloned.1.call-done = f32[8,256]{1,0:T(8,128)} async-done(((f32[8,8192]{1,0:T(8,128)}), f32[8,256]{1,0:T(8,128)}) %reduce-scatter.9.cloned.1.call-update) | async-done | bytes 8208 | tf_op jit(solution)/shard_map/reduce_scatter | solution.py:59
  752.3 1.0 multiply_reduce_fusion
  753.4 101.7 %psum.31 = f32[8]{0:T(128)S(1)} all-reduce(f32[8]{0:T(128)S(1)} %get-tuple-element.13), channel_id=1, replica_groups=mesh['row'=32,'col'=16] {'row','col'}, use_global_device_ids=true, to_apply=%region_11.14 | all-reduce | flops 8 | bytes 64 | tf_op jit(solution)/shard_map/psum | solution.py:82
  855.1 0.7 multiply_subtract_fusion
  (23 shorter events, 0.1 us)
Async XLA Ops:
  7.2 63.8 %copy-start = (bf16[1,1,32,128,128]{4,3,2,1,0:T(8,128)(2,1)S(1)}, bf16[1,1,32,128,128]{4,3,2,1,0:T(8,128)(2,1)}, u32[]{:S(2)}) copy-start(bf16[1,1,32,128,128]{4,3,2,1,0:T(8,128)(2,1)} %param.15) | copy-start | bytes 3145732
  7.2 0.8 copy-start.4
  7.2 2.2 copy-start.1
  7.2 135.8 %reduce-scatter.7.cloned.1.call-start = ((), (), s32[]{:S(2)}) async-start(), calls=%async_computation.5 | async-start | bytes 139264 | tf_op jit(solution)/shard_map/reduce_scatter | solution.py:69
  72.0 0.7 copy-start.3
  73.6 191.0 %reduce-scatter.5.cloned.1.call-start = ((), (), s32[]{:S(2)}) async-start(), calls=%async_computation.4 | async-start | bytes 270336 | tf_op jit(solution)/shard_map/reduce_scatter | solution.py:59
  113.1 0.7 copy-start.2
  113.1 0.9 copy-start.5
  113.1 517.5 %reduce-scatter.11.cloned.1.call-start = ((), (), s32[]{:S(2)}) async-start(), calls=%async_computation.7 | async-start | bytes 139264 | tf_op jit(solution)/shard_map/reduce_scatter | solution.py:69
  114.0 150.6 %copy-start.6 = (f32[256]{0:T(256)S(1)}, f32[256]{0:T(256)}, u32[]{:S(2)}) copy-start(f32[256]{0:T(256)} %param.13) | copy-start | bytes 3076
  562.4 189.9 %reduce-scatter.9.cloned.1.call-start = ((), (), s32[]{:S(2)}) async-start(), calls=%async_computation.6 | async-start | bytes 270336 | tf_op jit(solution)/shard_map/reduce_scatter | solution.py:59
Sparse Core Ops, SparseCore 0:
  73.7 69.1 reduce-scatter.6
  147.3 117.2 reduce-scatter.4
  562.5 68.0 reduce-scatter.10
  634.8 117.4 reduce-scatter.8
where the time goes:
time: 863 us; the launch traced here: 862 us
  blocking collectives  492 us (57%)
  waiting for transfers between devices  337 us (39%)
  between operations  14.6 us (2%)
  matrix products  9.38 us (1%)
    reduce_scatter x2, waiting for transfers between devices, local(): lax.psum_scatter(row_terms.reshape(rhs_count, row_devices * piece_len), '...  243 us
    psum x2, blocking collectives, residual_norms(): return lax.psum(jnp.sum(residual * residual, axis=1), ('row', 'col'))  202 us
    all_gather x2, blocking collectives, local(): by_row = lax.all_gather(masked, 'row', axis=1, tiled=True)  118 us
    psum x1, blocking collectives, local(): lax.psum(jnp.sum(direction * image_field, axis=1), ('row', 'col'))  102 us
    reduce_scatter x2, waiting for transfers between devices, local(): lax.psum_scatter(col_terms.reshape(rhs_count, col_devices * piece_len), '...  93.6 us
    all_gather x2, blocking collectives, local(): by_col = lax.all_gather(masked, 'col', axis=1, tiled=True)  69.9 us
  transfers between devices with their start and end apart: 4, of which 4 were waited for; matrix products, arithmetic and copies ran while one was open for 1% of the time, Pallas kernels for 0%

commit v1 on v0

--- a/solution.py
+++ b/solution.py
@@ -79,7 +79,9 @@
         )
         total = own_rows + mirrored + diag_terms.reshape(rhs_count, piece_len)
         image_field = noise_row * direction + observed_float * (coupling * total)
-        step_alpha = norm_now / lax.psum(jnp.sum(direction * image_field, axis=1), ("row", "col"))
+        step_alpha = norm_now / lax.psum(
+            lax.psum(jnp.sum(direction * image_field, axis=1), "row"), "col"
+        )
         solution = solution + step_alpha[:, None] * direction
         residual = residual - step_alpha[:, None] * image_field
         norm_next = residual_norms(residual)

time: 863 us -> 1010 us (1.17)
  blocking collectives: 492 us -> 636 us
    psum x1 -> x4, blocking collectives: 102 us -> 239 us  [the longest x2 173 us: local(): lax.psum(jnp.sum(direction * image_field, axis=1), 'row')]
where the time goes in v1:
time: 1010 us
  blocking collectives  636 us (63%)
  waiting for transfers between devices  337 us (33%)
  between operations  14.6 us (1%)
    reduce_scatter x2, waiting for transfers between devices, local(): lax.psum_scatter(row_terms.reshape(rhs_count, row_devices * piece_len), '...  243 us
    psum x2, blocking collectives, residual_norms(): return lax.psum(jnp.sum(residual * residual, axis=1), ('row', 'col'))  208 us
    psum x2, blocking collectives, local(): lax.psum(jnp.sum(direction * image_field, axis=1), 'row')  173 us
    all_gather x2, blocking collectives, local(): by_row = lax.all_gather(masked, 'row', axis=1, tiled=True)  119 us
    reduce_scatter x2, waiting for transfers between devices, local(): lax.psum_scatter(col_terms.reshape(rhs_count, col_devices * piece_len), '...  93.6 us
    all_gather x2, blocking collectives, local(): by_col = lax.all_gather(masked, 'col', axis=1, tiled=True)  69.9 us
    psum x2, blocking collectives, local(): lax.psum(lax.psum(jnp.sum(direction * image_field, axis=1), 'row'), 'col')  66.6 us
  transfers between devices with their start and end apart: 4, of which 4 were waited for; matrix products, arithmetic and copies ran while one was open for 1% of the time, Pallas kernels for 0%

profile of v1, /device:TPU:1, one launch (start us, length us, event | category | flops | bytes accessed | tf_op | source)
XLA Modules:
  0.0 1006.1 jit_solution(18148739617973903369)
XLA Ops:
  7.2 0.0 reduce-scatter.7.cloned.1.call-start
  7.2 0.7 compare_select_fusion
  8.0 0.7 convert_element_type.4
  9.4 61.0 %all_gather.13 = f32[8,8192]{1,0:T(8,128)S(1)} all-gather(f32[8,256]{1,0:T(8,128)S(1)} %broadcast_multiply_fusion.1), channel_id=1, replica_groups=mesh['row'=32,'col'=16] {'row'}, dimensions={1}, use_global_device_ids=true | all-gather | bytes 270336 | tf_op jit(solution)/shard_map/all_gather | solution.py:52
  70.4 0.6 gather_fusion.1
  71.0 1.0 fusion.12
  72.0 0.7 copy-done.3
  72.7 0.2 convolution_bitcast_fusion.3
  72.9 0.7 copy.41
  73.6 0.0 reduce-scatter.7.cloned.1.call-update
  73.6 0.0 reduce-scatter.5.cloned.1.call-start
  73.7 35.8 %all_gather.12 = f32[8,4096]{1,0:T(8,128)S(1)} all-gather(f32[8,256]{1,0:T(8,128)S(1)} %broadcast_multiply_fusion.1), channel_id=1, replica_groups=mesh['row'=32,'col'=16] {'col'}, dimensions={1}, use_global_device_ids=true | all-gather | bytes 139264 | tf_op jit(solution)/shard_map/all_gather | solution.py:51
  109.5 0.6 gather_fusion
  110.1 1.8 fusion.14
  111.8 0.4 convolution_bitcast_fusion.1
  112.2 0.8 copy.39
  113.1 0.0 reduce-scatter.5.cloned.1.call-update
  113.1 0.0 reduce-scatter.11.cloned.1.call-start
  113.2 0.6 copy-done.2
  113.8 0.1 copy-done.5
  114.0 0.3 fusion.17
  114.2 28.7 %reduce-scatter.7.cloned.1.call-done = f32[8,256]{1,0:T(8,128)} async-done(((f32[8,4096]{1,0:T(8,128)}), f32[8,256]{1,0:T(8,128)}) %reduce-scatter.7.cloned.1.call-update) | async-done | bytes 8208 | tf_op jit(solution)/shard_map/reduce_scatter | solution.py:69
  143.0 121.6 %reduce-scatter.5.cloned.1.call-done = f32[8,256]{1,0:T(8,128)} async-done(((f32[8,8192]{1,0:T(8,128)}), f32[8,256]{1,0:T(8,128)}) %reduce-scatter.5.cloned.1.call-update) | async-done | bytes 8208 | tf_op jit(solution)/shard_map/reduce_scatter | solution.py:59
  264.6 1.1 multiply_reduce_fusion.2
  265.7 86.3 %psum.43 = f32[8]{0:T(128)S(1)} all-reduce(f32[8]{0:T(128)S(1)} %get-tuple-element.4), channel_id=1, replica_groups=mesh['row'=32,'col'=16] {'row'}, use_global_device_ids=true, to_apply=%region_5.8 | all-reduce | flops 8 | bytes 64 | tf_op jit(solution)/shard_map/psum | solution.py:83
  352.0 102.3 %psum.42 = f32[8]{0:T(128)S(1)} all-reduce(f32[8]{0:T(128)S(1)} %get-tuple-element.5), channel_id=1, replica_groups=mesh['row'=32,'col'=16] {'row','col'}, use_global_device_ids=true, to_apply=%region_1.2 | all-reduce | flops 8 | bytes 64 | tf_op jit(solution)/shard_map/psum | solution.py:13
  454.2 32.8 %psum.44 = f32[8]{0:T(128)S(1)} all-reduce(f32[8]{0:T(128)S(1)} %psum.43), channel_id=1, replica_groups=mesh['row'=32,'col'=16] {'col'}, use_global_device_ids=true, to_apply=%region_6.9 | all-reduce | flops 8 | bytes 64 | tf_op jit(solution)/shard_map/psum | solution.py:82
  487.0 0.2 multiply_reduce_fusion.1
  487.2 105.6 %psum.45 = f32[8]{0:T(128)S(1)} all-reduce(f32[8]{0:T(128)S(1)} %multiply_reduce_fusion.1), channel_id=1, replica_groups=mesh['row'=32,'col'=16] {'row','col'}, use_global_device_ids=true, to_apply=%region_8.11 | all-reduce | flops 8 | bytes 64 | tf_op jit(solution)/shard_map/psum | solution.py:13
  592.8 0.1 broadcast_multiply_fusion
  592.9 34.1 %all_gather.14 = f32[8,4096]{1,0:T(8,128)S(1)} all-gather(f32[8,256]{1,0:T(8,128)S(1)} %get-tuple-element.6), channel_id=1, replica_groups=mesh['row'=32,'col'=16] {'col'}, dimensions={1}, use_global_device_ids=true | all-gather | bytes 139264 | tf_op jit(solution)/shard_map/all_gather | solution.py:51
  627.0 57.5 %all_gather.15 = f32[8,8192]{1,0:T(8,128)S(1)} all-gather(f32[8,256]{1,0:T(8,128)S(1)} %get-tuple-element.6), channel_id=1, replica_groups=mesh['row'=32,'col'=16] {'row'}, dimensions={1}, use_global_device_ids=true | all-gather | bytes 270336 | tf_op jit(solution)/shard_map/all_gather | solution.py:52
  684.5 0.6 gather_fusion.2
  685.1 0.6 gather_fusion.3
  685.7 1.0 fusion.8
  686.7 0.2 convolution_bitcast_fusion.2
  686.9 0.7 copy.40
  687.7 0.0 reduce-scatter.9.cloned.1.call-start
  687.7 1.8 fusion.10
  689.5 0.4 convolution_bitcast_fusion
  689.9 0.8 copy.38
  690.8 0.3 fusion.16
  691.0 64.9 %reduce-scatter.11.cloned.1.call-done = f32[8,256]{1,0:T(8,128)} async-done(((f32[8,4096]{1,0:T(8,128)}), f32[8,256]{1,0:T(8,128)}) %reduce-scatter.11.cloned.1.call-update) | async-done | bytes 8208 | tf_op jit(solution)/shard_map/reduce_scatter | solution.py:69
  755.9 121.6 %reduce-scatter.9.cloned.1.call-done = f32[8,256]{1,0:T(8,128)} async-done(((f32[8,8192]{1,0:T(8,128)}), f32[8,256]{1,0:T(8,128)}) %reduce-scatter.9.cloned.1.call-update) | async-done | bytes 8208 | tf_op jit(solution)/shard_map/reduce_scatter | solution.py:59
  877.6 1.0 multiply_reduce_fusion
  878.6 86.3 %psum.46 = f32[8]{0:T(128)S(1)} all-reduce(f32[8]{0:T(128)S(1)} %get-tuple-element.11), channel_id=1, replica_groups=mesh['row'=32,'col'=16] {'row'}, use_global_device_ids=true, to_apply=%region_12.15 | all-reduce | flops 8 | bytes 64 | tf_op jit(solution)/shard_map/psum | solution.py:83
  965.0 33.9 %psum.47 = f32[8]{0:T(128)S(1)} all-reduce(f32[8]{0:T(128)S(1)} %psum.46), channel_id=1, replica_groups=mesh['row'=32,'col'=16] {'col'}, use_global_device_ids=true, to_apply=%region_13.16 | all-reduce | flops 8 | bytes 64 | tf_op jit(solution)/shard_map/psum | solution.py:82
  998.8 0.7 multiply_subtract_fusion
  (26 shorter events, 0.2 us)
Async XLA Ops:
  7.2 63.8 %copy-start = (bf16[1,1,32,128,128]{4,3,2,1,0:T(8,128)(2,1)S(1)}, bf16[1,1,32,128,128]{4,3,2,1,0:T(8,128)(2,1)}, u32[]{:S(2)}) copy-start(bf16[1,1,32,128,128]{4,3,2,1,0:T(8,128)(2,1)} %param.15) | copy-start | bytes 3145732
  7.2 0.8 copy-start.4
  7.2 2.2 copy-start.1
  7.2 135.8 %reduce-scatter.7.cloned.1.call-start = ((), (), s32[]{:S(2)}) async-start(), calls=%async_computation.5 | async-start | bytes 139264 | tf_op jit(solution)/shard_map/reduce_scatter | solution.py:69
  72.0 0.7 copy-start.3
  73.6 191.0 %reduce-scatter.5.cloned.1.call-start = ((), (), s32[]{:S(2)}) async-start(), calls=%async_computation.4 | async-start | bytes 270336 | tf_op jit(solution)/shard_map/reduce_scatter | solution.py:59
  113.1 0.7 copy-start.2
  113.1 0.9 copy-start.5
  113.1 642.8 %reduce-scatter.11.cloned.1.call-start = ((), (), s32[]{:S(2)}) async-start(), calls=%async_computation.7 | async-start | bytes 139264 | tf_op jit(solution)/shard_map/reduce_scatter | solution.py:69
  114.0 150.6 %copy-start.6 = (f32[256]{0:T(256)S(1)}, f32[256]{0:T(256)}, u32[]{:S(2)}) copy-start(f32[256]{0:T(256)} %param.13) | copy-start | bytes 3076
  687.7 189.9 %reduce-scatter.9.cloned.1.call-start = ((), (), s32[]{:S(2)}) async-start(), calls=%async_computation.6 | async-start | bytes 270336 | tf_op jit(solution)/shard_map/reduce_scatter | solution.py:59
Sparse Core Ops, SparseCore 0:
  73.7 69.1 reduce-scatter.6
  147.3 117.2 reduce-scatter.4
  687.8 68.1 reduce-scatter.10
  760.1 117.4 reduce-scatter.8
